TPU v7x, 128 devices: a whole 4x4x4 slice. The times are simulated.
128 devices in a mesh: group: 4 (over x), bulk: 32 (over z, y, core).
Axes of the slice: x: 4, y: 4, z: 4, core: 2. Of those that a mesh axis runs over, the one named last changes fastest.
Arguments:
- rhs: float32 [512, 64, 128], P(('group', 'bulk')), may hold values from -90 to 90, as said below
- diag_tiles: float32 [512, 128, 128], P(('group', 'bulk')), may hold values from -0.06 to 0.06
- offdiag_blocks: float32 [512, 11, 128, 128], P(('group', 'bulk')), may hold values from -0.026 to 0.026
- coupling: float32 [256, 4, 128, 128], P(('group', 'bulk')), may hold values from -0.05 to 0.05, as said below
- col_index: int32 [512, 11], replicated, may hold values from 0 to 511, as said below
- load: int32 [512], replicated, may hold values from 3 to 11
- new_slot: int32 [512], replicated, may hold values from 0 to 511, as said below
Outputs:
- solution_out: float32 [512, 64, 128], P(('group', 'bulk'))
- residual_out: float32 [512, 64, 128], P(('group', 'bulk'))
Inputs may be any that keep to these rules, and one draw needn't show every extreme that they name: `rhs`: made of random entries times scales of the rows and of the columns. `coupling`: entry [d * 2 + k, h] is the transpose of entry [(h * 32 + d % 32) * 2 + k, d // 32]. `col_index`: for each part g and each tile position t, the column t of the 128 block rows of part g is a permutation of that part's slots g * 128 to (g + 1) * 128 - 1. Of the 44 entries of the 4 block rows of one device (slots d * 4 to (d + 1) * 4 - 1), at most 2 name slots of any one device, and exactly 2 name slots of some device. `new_slot`: A permutation. On every device exactly one block row moves, from a slot k with 2 <= k % 4; it stays in its part, goes from owner b to owner b XOR m, where m (1 to 31) is one number for the whole part, and takes the slot that the moving row of that device leaves.
All inputs are finite; a program needn't handle non-finite values.
Results may differ from a plain program's by a relative error of at most 0.0003.
Values sent between devices are 32-bit elements; how exact they have to be, the bound alone decides.
A program may use at most 64 MiB of HBM per device.

v0:
```python
import jax
import jax.numpy as jnp
from jax import lax
from jax.sharding import PartitionSpec as P

highest = lax.Precision.HIGHEST
diagonal_shift = 4.0


def chol_apply(matrix, right):
    factor = jnp.linalg.cholesky(matrix)
    middle = lax.linalg.triangular_solve(factor, right, left_side=True, lower=True)
    return lax.linalg.triangular_solve(factor, middle, left_side=True, lower=True, transpose_a=True)


def gram(left, right):
    return jnp.einsum("snt,smt->nm", left, right, precision=highest)


def sym(m):
    return 0.5 * (m + m.T)


def mm(a, b):
    return jnp.dot(a, b, precision=highest)


def off_part(vectors, diag, masked, column_ids, coupling):
    boundary_rows = coupling.shape[0]
    part_count = coupling.shape[1]
    border = lax.all_gather(vectors[:boundary_rows], "group", axis=0, tiled=True)
    own = jnp.einsum("rnj,rij->rni", vectors, diag, precision=highest)
    returned = jnp.einsum("rni,rkij->rknj", vectors, masked, precision=highest)
    panel = lax.all_gather(vectors, "bulk", axis=0, tiled=True)
    picked = panel[column_ids]
    own = own + jnp.einsum("rknj,rkij->rni", picked, masked, precision=highest)
    border = border.reshape((part_count, boundary_rows) + vectors.shape[1:])
    crossed = jnp.einsum("khij,hknj->kni", coupling, border, precision=highest)
    return (own.at[:boundary_rows].add(crossed), returned.reshape((-1,) + vectors.shape[1:]), panel)


def coefficients(n0, n1, n2, n3):
    n = n0.shape[0]
    eye = jnp.eye(n, dtype=n0.dtype)
    n0, n1, n2, n3 = (sym(n0), sym(n1), sym(n2), sym(n3))
    delta = chol_apply(diagonal_shift * n0 + n1, n1)
    alpha = (eye - delta) / diagonal_shift
    b = -alpha
    cross = mm(delta.T, mm(n1, b))
    gram_new = sym(mm(delta.T, mm(n0, delta)) + cross + cross.T + mm(b.T, mm(n2, b)))
    beta = chol_apply(n0, gram_new)
    a = delta + beta
    c1 = mm(a.T, mm(n1, b))
    c2 = mm(a.T, mm(n2, b))
    pp = mm(a.T, mm(n0, a)) + c1 + c1.T + mm(b.T, mm(n2, b))
    pep = mm(a.T, mm(n1, a)) + c2 + c2.T + mm(b.T, mm(n3, b))
    alpha2 = chol_apply(sym(diagonal_shift * pp + pep), gram_new)
    ba = mm(b, alpha2)
    aa = mm(a, alpha2)
    sol = (alpha + aa, ba)
    res = (delta - diagonal_shift * aa, b - diagonal_shift * ba - aa, -ba)
    return (sol, res)


def local(rhs, diag_tiles, offdiag_blocks, coupling, col_index, load, new_slot):
    row_count = rhs.shape[0]
    off_count = offdiag_blocks.shape[1]
    bulk_count = lax.axis_size("bulk")
    group_rows = row_count * bulk_count
    group_base = lax.axis_index("group") * group_rows
    first = lax.axis_index("bulk") * row_count
    cols = lax.dynamic_slice_in_dim(col_index, group_base, group_rows) - group_base
    moved = lax.dynamic_slice_in_dim(new_slot, group_base, group_rows) - group_base
    loads = lax.dynamic_slice_in_dim(load, group_base + first, row_count)
    my_cols = lax.dynamic_slice_in_dim(cols, first, row_count)
    my_new = lax.dynamic_slice_in_dim(moved, first, row_count)
    tile_ids = jnp.arange(off_count, dtype=jnp.int32)
    mask = (tile_ids[None, :] < loads[:, None]).astype(jnp.float32)
    masked = offdiag_blocks * mask[:, :, None, None]
    u0 = rhs
    own, returned, panel0 = off_part(u0, diag_tiles, masked, my_cols, coupling)
    buffer = jax.ops.segment_sum(returned, my_cols.reshape(-1), num_segments=group_rows)
    u1 = own + lax.psum_scatter(buffer, "bulk", scatter_dimension=0, tiled=True)
    own, returned, panel1 = off_part(u1, diag_tiles, masked, my_cols, coupling)
    ids = jnp.concatenate([moved[my_cols.reshape(-1)], my_new])
    buffer = jax.ops.segment_sum(jnp.concatenate([returned, own]), ids, num_segments=group_rows)
    u2 = lax.psum_scatter(buffer, "bulk", scatter_dimension=0, tiled=True)
    inverse = jnp.zeros_like(moved).at[moved].set(jnp.arange(group_rows, dtype=jnp.int32))
    mine = lax.dynamic_slice_in_dim(inverse, first, row_count)
    v0, v1 = (panel0[mine], panel1[mine])
    grams = jnp.stack([gram(v0, v0), gram(v0, v1), gram(v1, v1), gram(v1, u2)])
    grams = lax.psum(grams, ("group", "bulk"))
    sol, res = coefficients(grams[0], grams[1], grams[2], grams[3])
    basis = jnp.concatenate([v0, v1, u2], axis=1)
    zero = jnp.zeros_like(sol[0])
    weights = jnp.concatenate(
        [jnp.concatenate(sol + (zero,), axis=0), jnp.concatenate(res, axis=0)], axis=1
    )
    out = jnp.einsum("mn,smt->snt", weights, basis, precision=highest)
    n = rhs.shape[1]
    return (out[:, :n], out[:, n:])


def solution(mesh):
    return jax.shard_map(
        local,
        mesh=mesh,
        in_specs=(
            P(("group", "bulk"), None, None),
            P(("group", "bulk"), None, None),
            P(("group", "bulk"), None, None, None),
            P(("group", "bulk"), None, None, None),
            P(),
            P(),
            P(),
        ),
        out_specs=(P(("group", "bulk"), None, None), P(("group", "bulk"), None, None)),
        check_vma=False,
    )
```

profile of v0, /device:TPU:1, one launch (start us, length us, event | category | flops | bytes accessed | tf_op | source)
XLA Modules:
  0.0 494.6 jit_solution(10182201475086260046)
XLA Ops:
  7.2 0.7 all-gather.3.cloned.1.call-update
  8.0 0.8 compare_select_fusion
  8.9 0.8 dynamic_slice.22
  9.8 3.8 fusion.4
  13.5 2.5 broadcast.140.clone
  16.0 6.9 %scatter_fusion = f32[128,64,128]{2,1,0:T(8,128)} fusion(f32[128,64,128]{2,1,0:T(8,128)} %broadcast.140.clone, s32[44]{0:T(128)S(1)} %reshape.206, f32[44,64,128]{2,1,0:T(8,128)S(1)} %bitcast.248), kind=kCustom, calls=%fused_computation.6 | custom fusion | flops 360448 | bytes 4325552 | tf_op jit(solution)/shard_map/scatter-add | solution.py:82
  23.0 0.8 copy-done.4
  23.8 0.6 slice.81
  24.4 0.7 copy.72
  25.1 0.8 reshape.166
  25.9 12.7 %all_gather.13 = f32[8,64,128]{2,1,0:T(8,128)} all-gather(f32[2,64,128]{2,1,0:T(8,128)} %slice.81), channel_id=1, replica_groups=mesh['group'=4,'bulk'=32] {'group'}, dimensions={0}, use_global_device_ids=true | all-gather | bytes 327680 | tf_op jit(solution)/shard_map/all_gather | solution.py:31
  38.5 21.5 %all-gather.3.cloned.1.call-done = f32[128,64,128]{2,1,0:T(8,128)} async-done(((f32[4,64,128]{2,1,0:T(8,128)}), f32[128,64,128]{2,1,0:T(8,128)}) %all-gather.3.cloned.1.call-update) | async-done | bytes 4194320 | tf_op jit(solution)/shard_map/all_gather | solution.py:34
  60.1 4.0 gather_fusion.1
  64.1 4.8 fusion.12
  68.9 1.3 convolution_add_fusion.1
  70.2 2.1 fusion.21
  72.4 71.0 %reduce-scatter.3.cloned.1.call-done = f32[4,64,128]{2,1,0:T(8,128)} async-done(((f32[128,64,128]{2,1,0:T(8,128)}), f32[4,64,128]{2,1,0:T(8,128)}) %reduce-scatter.3.cloned.1.call-update) | async-done | bytes 131088 | tf_op jit(solution)/shard_map/reduce_scatter | solution.py:83
  143.4 1.6 add.181
  145.2 0.8 compare_select_fusion.3
  146.0 0.8 gather_fusion.3
  146.9 0.8 slice.102
  147.7 10.6 %all_gather.15 = f32[8,64,128]{2,1,0:T(8,128)} all-gather(f32[2,64,128]{2,1,0:T(8,128)S(1)} %slice.102), channel_id=1, replica_groups=mesh['group'=4,'bulk'=32] {'group'}, dimensions={0}, use_global_device_ids=true | all-gather | bytes 327680 | tf_op jit(solution)/shard_map/all_gather | solution.py:31
  158.3 4.1 fusion.2
  162.4 31.4 %all-gather.5.cloned.1.call-done = f32[128,64,128]{2,1,0:T(8,128)} async-done(((f32[4,64,128]{2,1,0:T(8,128)}), f32[128,64,128]{2,1,0:T(8,128)}) %all-gather.5.cloned.1.call-update) | async-done | bytes 4194320 | tf_op jit(solution)/shard_map/all_gather | solution.py:34
  193.8 3.9 gather_fusion.4
  197.7 4.9 fusion.15
  202.7 0.6 convolution_add_fusion
  203.3 0.7 fusion.19
  204.1 2.5 broadcast.140
  206.6 6.9 %scatter_fusion.1 = f32[128,64,128]{2,1,0:T(8,128)} fusion(f32[128,64,128]{2,1,0:T(8,128)} %broadcast.140, s32[48]{0:T(128)S(1)} %pad_add_fusion, f32[48,64,128]{2,1,0:T(8,128)S(1)} %pad_maximum_fusion), kind=kCustom, calls=%fused_computation.7 | custom fusion | flops 393216 | bytes 4718784 | tf_op jit(solution)/shard_map/scatter-add | solution.py:86
  213.6 1.2 scatter_custom_fusion
  214.9 2.7 gather_fusion
  217.6 0.3 convolution_bitcast_fusion.6
  217.9 2.7 gather_fusion.2
  220.6 0.3 convolution_bitcast_fusion.4
  220.9 0.3 convolution_bitcast_fusion.5
  221.1 72.2 %reduce-scatter.5.cloned.1.call-done = f32[4,64,128]{2,1,0:T(8,128)} async-done(((f32[128,64,128]{2,1,0:T(8,128)}), f32[4,64,128]{2,1,0:T(8,128)}) %reduce-scatter.5.cloned.1.call-update) | async-done | bytes 131088 | tf_op jit(solution)/shard_map/reduce_scatter | solution.py:87
  293.4 1.2 convolution_bitcast_fusion.3
  294.5 0.7 pad_maximum_fusion.1
  295.2 146.3 %all-reduce.2.cloned.1.call-done = f32[4,64,64]{2,1,0:T(8,128)} async-done(((f32[4,64,64]{2,1,0:T(8,128)}), f32[4,64,64]{2,1,0:T(8,128)}) %all-reduce.2.cloned.1.call-update) | async-done | bytes 65552 | tf_op jit(solution)/shard_map/psum | solution.py:92
  441.6 0.8 slice_bitcast_fusion.2
  442.5 0.8 multiply_add_fusion
  443.6 5.9 %cholesky.59 = f32[64,64]{1,0:T(8,128)S(1)} custom-call(f32[64,64]{1,0:T(8,128)S(1)} %copy.82), custom_call_target="Cholesky" | custom-call | tf_op jit(solution)/shard_map/jit(cholesky)/cholesky | solution.py:11
  449.5 0.6 compare_reduce_fusion.2
  450.1 0.7 fusion.41
  450.8 4.9 custom-call.13
  455.7 0.3 fusion.74
  456.0 0.2 fusion.76
  456.7 5.9 %cholesky.70 = f32[64,64]{1,0:T(8,128)S(1)} custom-call(f32[64,64]{1,0:T(8,128)S(1)} %copy.85), custom_call_target="Cholesky" | custom-call | tf_op jit(solution)/shard_map/jit(cholesky)/cholesky | solution.py:11
  462.6 0.6 compare_reduce_fusion.1
  463.3 0.7 fusion.42
  463.9 4.9 custom-call.15
  468.8 1.0 fusion.67
  470.8 0.2 convolution_add_fusion.2
  471.9 1.0 fusion.45
  473.9 5.8 %cholesky.81 = f32[64,64]{1,0:T(8,128)S(1)} custom-call(f32[64,64]{1,0:T(8,128)S(1)} %fusion.51), custom_call_target="Cholesky" | custom-call | tf_op jit(solution)/shard_map/jit(cholesky)/cholesky | solution.py:11
  479.8 0.6 compare_reduce_fusion
  480.5 0.7 fusion.43
  481.1 4.9 custom-call.17
  486.0 0.2 fusion.47
  486.4 0.2 fusion.92
  486.7 0.2 fusion.81
  487.0 0.4 convolution_bitcast_fusion
  487.4 0.7 fusion.103
  (80 shorter events, 4.9 us)
Async XLA Ops:
  7.2 63.1 %copy-start = (f32[2,4,128,128]{3,2,1,0:T(8,128)S(1)}, f32[2,4,128,128]{3,2,1,0:T(8,128)}, u32[]{:S(2)}) copy-start(f32[2,4,128,128]{3,2,1,0:T(8,128)} %param.19) | copy-start | bytes 1572868
  7.2 52.9 %all-gather.3.cloned.1.call-start = ((), (), s32[]{:S(2)}) async-start(), calls=%async_computation.2 | async-start | bytes 4325376 | tf_op jit(solution)/shard_map/all_gather | solution.py:34
  7.9 135.5 %reduce-scatter.3.cloned.1.call-start = ((), (), s32[]{:S(2)}) async-start(), calls=%async_computation.3 | async-start | bytes 4325376 | tf_op jit(solution)/shard_map/reduce_scatter | solution.py:83
  22.9 0.9 copy-start.4
  22.9 41.2 %copy-start.1 = (f32[4,11,128,128]{3,2,1,0:T(8,128)S(1)}, f32[4,11,128,128]{3,2,1,0:T(8,128)}, u32[]{:S(2)}) copy-start(f32[4,11,128,128]{3,2,1,0:T(8,128)} %param.18) | copy-start | bytes 8650756
  22.9 170.9 %all-gather.5.cloned.1.call-start = ((), (), s32[]{:S(2)}) async-start(), calls=%async_computation.4 | async-start | bytes 4325376 | tf_op jit(solution)/shard_map/all_gather | solution.py:34
  64.1 4.8 copy-start.7
  64.1 6.1 %copy-start.6 = (f32[8,64,128]{2,1,0:T(8,128)S(1)}, f32[8,64,128]{2,1,0:T(8,128)}, u32[]{:S(2)}) copy-start(f32[8,64,128]{2,1,0:T(8,128)} %all_gather.13) | copy-start | bytes 786436
  145.0 148.3 %reduce-scatter.5.cloned.1.call-start = ((), (), s32[]{:S(2)}) async-start(), calls=%async_computation.5 | async-start | bytes 4325376 | tf_op jit(solution)/shard_map/reduce_scatter | solution.py:87
  197.7 4.9 copy-start.3
  197.7 4.9 %copy-start.8 = (f32[4,128,128]{2,1,0:T(8,128)S(1)}, f32[4,128,128]{2,1,0:T(8,128)}, u32[]{:S(2)}) copy-start(f32[4,128,128]{2,1,0:T(8,128)} %param.17) | copy-start | bytes 786436
  197.7 5.6 %copy-start.5 = (f32[8,64,128]{2,1,0:T(8,128)S(1)}, f32[8,64,128]{2,1,0:T(8,128)}, u32[]{:S(2)}) copy-start(f32[8,64,128]{2,1,0:T(8,128)} %all_gather.15) | copy-start | bytes 786436
  197.7 6.2 %copy-start.2 = (f32[4,11,128,64]{2,3,1,0:T(8,128)S(1)}, f32[4,11,128,64]{2,3,1,0:T(8,128)}, u32[]{:S(2)}) copy-start(f32[4,11,128,64]{2,3,1,0:T(8,128)} %fusion.2) | copy-start | bytes 4325380
  213.5 228.1 %all-reduce.2.cloned.1.call-start = ((), (), s32[]{:S(2)}) async-start(), calls=%async_computation.6 | async-start | bytes 262144 | tf_op jit(solution)/shard_map/psum | solution.py:92
  294.5 192.4 %copy-start.9 = (f32[4,64,128]{2,1,0:T(8,128)S(1)}, f32[4,64,128]{2,1,0:T(8,128)}, u32[]{:S(2)}) copy-start(f32[4,64,128]{2,1,0:T(8,128)} %reduce-scatter.5.cloned.1.call-done) | copy-start | bytes 393220
Sparse Core Ops, SparseCore 0:
  10.2 49.7 all-gather.2
  63.7 79.6 reduce-scatter.2
  146.2 47.5 all-gather.4
  213.6 79.7 reduce-scatter.4
  298.5 142.9 all-reduce.1
where the time goes:
time: 496 us; the launch traced here: 495 us
  waiting for transfers between devices  343 us (69%)
  other arithmetic  55.1 us (11%)
  matrix products  30.5 us (6%)
  local copies, waits for them, and re-layouts  28.1 us (6%)
  blocking collectives  23.2 us (5%)
  between operations  14.3 us (3%)
    psum x1, waiting for transfers between devices, local(): grams = lax.psum(grams, ('group', 'bulk'))  146 us
    reduce_scatter x1, waiting for transfers between devices, local(): u2 = lax.psum_scatter(buffer, 'bulk', scatter_dimension=0, tiled=True)  72.2 us
    reduce_scatter x1, waiting for transfers between devices, local(): u1 = own + lax.psum_scatter(buffer, 'bulk', scatter_dimension=0, tiled=True)  71 us
    all_gather x2, waiting for transfers between devices, off_part(): panel = lax.all_gather(vectors, 'bulk', axis=0, tiled=True)  52.9 us
    all_gather x2, blocking collectives, off_part(): lax.all_gather(vectors[:boundary_rows], 'group', axis=0, tiled=True)  23.2 us
    another operation x9, other arithmetic, chol_apply(): factor = jnp.linalg.cholesky(matrix)  19.6 us
    another operation x6, other arithmetic, chol_apply(): lax.linalg.triangular_solve(factor, middle, left_side=True, lower=True, t...  16.6 us
  transfers between devices with their start and end apart: 5, of which 5 were waited for; matrix products, arithmetic and copies ran while one was open for 9% of the time, Pallas kernels for 0%

commit v1 on v0

--- a/solution.py
+++ b/solution.py
@@ -31,7 +31,9 @@
     border = lax.all_gather(vectors[:boundary_rows], "group", axis=0, tiled=True)
     own = jnp.einsum("rnj,rij->rni", vectors, diag, precision=highest)
     returned = jnp.einsum("rni,rkij->rknj", vectors, masked, precision=highest)
-    panel = lax.all_gather(vectors, "bulk", axis=0, tiled=True)
+    panel = jnp.concatenate(
+        lax.all_to_all(jnp.stack([vectors] * lax.axis_size("bulk")), "bulk", 0, 0), axis=0
+    )
     picked = panel[column_ids]
     own = own + jnp.einsum("rknj,rkij->rni", picked, masked, precision=highest)
     border = border.reshape((part_count, boundary_rows) + vectors.shape[1:])

time: 496 us -> 480 us (0.968)
  waiting for transfers between devices: 343 us -> 305 us
  starting transfers between devices: 0.2 us -> 17.3 us
    all_to_all x0 -> x2, waiting for transfers between devices: none -> 73.7 us  [off_part(): lax.all_to_all(jnp.stack([vectors] * lax.axis_size('bulk')), 'bulk', 0, 0)]
    reduce_scatter x1, waiting for transfers between devices: 71 us -> 12.4 us  [local(): u1 = own + lax.psum_scatter(buffer, 'bulk', scatter_dimension=0, tiled=True)]
    all_gather x2 -> x0, waiting for transfers between devices: 52.9 us -> none  [off_part(): panel = lax.all_gather(vectors, 'bulk', axis=0, tiled=True)]
    all_to_all x0 -> x2, starting transfers between devices: none -> 17.2 us  [off_part(): lax.all_to_all(jnp.stack([vectors] * lax.axis_size('bulk')), 'bulk', 0, 0)]
    another operation x2 -> x4, local copies, waits for them, and re-layouts: 5 us -> 10 us
  transfers between devices with their start and end apart: 5 -> 5, of which waited for: 5 -> 5; matrix products, arithmetic and copies ran while one was open for 9% -> 6% of each run, Pallas kernels for 0% -> 0%
where the time goes in v1:
time: 480 us; the launch traced here: 479 us
  waiting for transfers between devices  305 us (64%)
  other arithmetic  55.6 us (12%)
  local copies, waits for them, and re-layouts  32.9 us (7%)
  matrix products  29.6 us (6%)
  blocking collectives  24 us (5%)
  starting transfers between devices  17.3 us (4%)
  between operations  14.3 us (3%)
    psum x1, waiting for transfers between devices, local(): grams = lax.psum(grams, ('group', 'bulk'))  147 us
    all_to_all x2, waiting for transfers between devices, off_part(): lax.all_to_all(jnp.stack([vectors] * lax.axis_size('bulk')), 'bulk', 0, 0)  73.7 us
    reduce_scatter x1, waiting for transfers between devices, local(): u2 = lax.psum_scatter(buffer, 'bulk', scatter_dimension=0, tiled=True)  72.6 us
    all_gather x2, blocking collectives, off_part(): lax.all_gather(vectors[:boundary_rows], 'group', axis=0, tiled=True)  24 us
    another operation x9, other arithmetic, chol_apply(): factor = jnp.linalg.cholesky(matrix)  19.6 us
    all_to_all x2, starting transfers between devices, off_part(): lax.all_to_all(jnp.stack([vectors] * lax.axis_size('bulk')), 'bulk', 0, 0)  17.2 us
    another operation x6, other arithmetic, chol_apply(): lax.linalg.triangular_solve(factor, middle, left_side=True, lower=True, t...  16.6 us
    reduce_scatter x1, waiting for transfers between devices, local(): u1 = own + lax.psum_scatter(buffer, 'bulk', scatter_dimension=0, tiled=True)  12.4 us
  transfers between devices with their start and end apart: 5, of which 5 were waited for; matrix products, arithmetic and copies ran while one was open for 6% of the time, Pallas kernels for 0%

profile of v1, /device:TPU:1, one launch (start us, length us, event | category | flops | bytes accessed | tf_op | source)
XLA Modules:
  0.0 478.9 jit_solution(547046562067172385)
XLA Ops:
  7.2 0.8 dynamic_slice.22
  8.1 0.8 compare_select_fusion
  9.0 0.6 copy-done.9
  9.6 3.8 fusion.4
  13.4 2.5 broadcast.144.clone
  15.9 6.9 %scatter_fusion = f32[128,64,128]{2,1,0:T(8,128)} fusion(f32[128,64,128]{2,1,0:T(8,128)} %broadcast.144.clone, s32[44]{0:T(128)S(1)} %reshape.218, f32[44,64,128]{2,1,0:T(8,128)S(1)} %bitcast.250), kind=kCustom, calls=%fused_computation.6 | custom fusion | flops 360448 | bytes 4325552 | tf_op jit(solution)/shard_map/scatter-add | solution.py:84
  22.8 0.9 copy-done.3
  23.7 2.5 stack.14
  26.2 9.7 %all-to-all-start = ((f32[32,4,64,128]{3,2,1,0:T(8,128)}), f32[32,4,64,128]{3,2,1,0:T(8,128)}, u32[]{:S(2)}, u32[]{:S(2)}) async-start(f32[32,4,64,128]{3,2,1,0:T(8,128)} %stack.14), calls=%async_computation | async-start | bytes 8388608 | tf_op jit(solution)/shard_map/all_to_all | solution.py:35
  35.9 0.6 slice.81
  36.7 12.6 %all_gather.6 = f32[8,64,128]{2,1,0:T(8,128)} all-gather(f32[2,64,128]{2,1,0:T(8,128)} %slice.81), channel_id=1, replica_groups=mesh['group'=4,'bulk'=32] {'group'}, dimensions={0}, use_global_device_ids=true | all-gather | bytes 327680 | tf_op jit(solution)/shard_map/all_gather | solution.py:31
  49.3 41.7 %all-to-all-done = f32[32,4,64,128]{3,2,1,0:T(8,128)} async-done(((f32[32,4,64,128]{3,2,1,0:T(8,128)}), f32[32,4,64,128]{3,2,1,0:T(8,128)}, u32[]{:S(2)}, u32[]{:S(2)}) %all-to-all-start) | async-done | bytes 4194336 | tf_op jit(solution)/shard_map/all_to_all | solution.py:35
  90.9 4.0 gather_fusion.1
  94.9 4.9 %fusion.12 = f32[4,64,128]{2,1,0:T(8,128)S(1)} fusion(f32[4,11,64,128]{3,2,1,0:T(8,128)} %bitcast.252, f32[4,11,128,128]{3,2,1,0:T(8,128)S(1)} %copy-done.1, f32[4,11]{1,0:T(4,128)S(1)} %fusion.85), kind=kOutput, calls=%fused_computation.22 | convolution fusion | flops 554369024 | bytes 4456624 | tf_op jit(solution)/shard_map/rknj,rkij->rni/dot_general | solution.py:38
  99.8 1.3 convolution_add_fusion.1
  101.1 2.1 fusion.21
  103.2 12.4 %reduce-scatter.3.cloned.1.call-done = f32[4,64,128]{2,1,0:T(8,128)} async-done(((f32[128,64,128]{2,1,0:T(8,128)}), f32[4,64,128]{2,1,0:T(8,128)}) %reduce-scatter.3.cloned.1.call-update) | async-done | bytes 131088 | tf_op jit(solution)/shard_map/reduce_scatter | solution.py:85
  115.6 1.0 add.181
  116.6 2.5 stack.15
  119.1 7.5 %all-to-all-start.1 = ((f32[32,4,64,128]{3,2,1,0:T(8,128)}), f32[32,4,64,128]{3,2,1,0:T(8,128)}, u32[]{:S(2)}, u32[]{:S(2)}) async-start(f32[32,4,64,128]{3,2,1,0:T(8,128)} %stack.15), calls=%async_computation.2 | async-start | bytes 8388608 | tf_op jit(solution)/shard_map/all_to_all | solution.py:35
  126.8 1.3 compare_select_fusion.3
  128.0 0.6 dynamic_slice.23
  128.6 1.3 gather_fusion.3
  130.0 0.7 pad_add_fusion
  130.7 11.5 %all_gather.7 = f32[8,64,128]{2,1,0:T(8,128)} all-gather(f32[2,64,128]{2,1,0:T(8,128)S(1)} %slice.102), channel_id=1, replica_groups=mesh['group'=4,'bulk'=32] {'group'}, dimensions={0}, use_global_device_ids=true | all-gather | bytes 327680 | tf_op jit(solution)/shard_map/all_gather | solution.py:31
  142.1 3.2 fusion.2
  145.3 32.0 %all-to-all-done.1 = f32[32,4,64,128]{3,2,1,0:T(8,128)} async-done(((f32[32,4,64,128]{3,2,1,0:T(8,128)}), f32[32,4,64,128]{3,2,1,0:T(8,128)}, u32[]{:S(2)}, u32[]{:S(2)}) %all-to-all-start.1) | async-done | bytes 4194336 | tf_op jit(solution)/shard_map/all_to_all | solution.py:35
  177.3 4.0 gather_fusion.4
  181.3 4.9 %fusion.15 = f32[4,64,128]{2,1,0:T(8,128)S(1)} fusion(f32[4,11,64,128]{3,2,1,0:T(8,128)} %bitcast.251, f32[4,11,128,128]{3,2,1,0:T(8,128)S(1)} %copy-done.1, f32[4,11]{1,0:T(4,128)S(1)} %fusion.85), kind=kOutput, calls=%fused_computation.23 | convolution fusion | flops 554369024 | bytes 4456624 | tf_op jit(solution)/shard_map/rknj,rkij->rni/dot_general | solution.py:38
  186.3 0.6 convolution_add_fusion
  186.9 0.7 fusion.19
  187.7 2.5 broadcast.144
  190.2 6.9 %scatter_fusion.1 = f32[128,64,128]{2,1,0:T(8,128)} fusion(f32[128,64,128]{2,1,0:T(8,128)} %broadcast.144, s32[48]{0:T(128)S(1)} %pad_add_fusion, f32[48,64,128]{2,1,0:T(8,128)S(1)} %pad_maximum_fusion), kind=kCustom, calls=%fused_computation.7 | custom fusion | flops 393216 | bytes 4718784 | tf_op jit(solution)/shard_map/scatter-add | solution.py:88
  197.2 1.3 scatter_custom_fusion
  198.6 2.7 gather_fusion
  201.3 0.3 convolution_bitcast_fusion.6
  201.6 2.7 gather_fusion.2
  204.3 0.3 convolution_bitcast_fusion.4
  204.6 0.3 convolution_bitcast_fusion.5
  204.9 72.6 %reduce-scatter.5.cloned.1.call-done = f32[4,64,128]{2,1,0:T(8,128)} async-done(((f32[128,64,128]{2,1,0:T(8,128)}), f32[4,64,128]{2,1,0:T(8,128)}) %reduce-scatter.5.cloned.1.call-update) | async-done | bytes 131088 | tf_op jit(solution)/shard_map/reduce_scatter | solution.py:89
  277.4 1.2 convolution_bitcast_fusion.3
  278.6 0.7 pad_maximum_fusion.1
  279.3 146.5 %all-reduce.2.cloned.1.call-done = f32[4,64,64]{2,1,0:T(8,128)} async-done(((f32[4,64,64]{2,1,0:T(8,128)}), f32[4,64,64]{2,1,0:T(8,128)}) %all-reduce.2.cloned.1.call-update) | async-done | bytes 65552 | tf_op jit(solution)/shard_map/psum | solution.py:94
  425.8 0.8 slice_bitcast_fusion.2
  426.8 0.8 multiply_add_fusion
  427.9 5.9 %cholesky.59 = f32[64,64]{1,0:T(8,128)S(1)} custom-call(f32[64,64]{1,0:T(8,128)S(1)} %copy.82), custom_call_target="Cholesky" | custom-call | tf_op jit(solution)/shard_map/jit(cholesky)/cholesky | solution.py:11
  433.8 0.6 compare_reduce_fusion.2
  434.4 0.7 fusion.41
  435.1 4.9 %custom-call.13 = f32[1,64,64]{1,2,0:T(8,128)S(1)} custom-call(f32[1,64,64]{2,1,0:T(8,128)S(1)} %fusion.41), custom_call_target="InvertDiagBlocksLowerTriangular" | custom-call | tf_op jit(solution)/shard_map/triangular_solve/custom-call.2 | solution.py:13
  440.0 0.3 fusion.74
  441.0 5.9 %cholesky.70 = f32[64,64]{1,0:T(8,128)S(1)} custom-call(f32[64,64]{1,0:T(8,128)S(1)} %copy.85), custom_call_target="Cholesky" | custom-call | tf_op jit(solution)/shard_map/jit(cholesky)/cholesky | solution.py:11
  446.9 0.6 compare_reduce_fusion.1
  447.6 0.7 fusion.42
  448.2 4.9 %custom-call.15 = f32[1,64,64]{1,2,0:T(8,128)S(1)} custom-call(f32[1,64,64]{2,1,0:T(8,128)S(1)} %fusion.42), custom_call_target="InvertDiagBlocksLowerTriangular" | custom-call | tf_op jit(solution)/shard_map/triangular_solve/custom-call.2 | solution.py:13
  453.1 1.0 fusion.67
  456.1 1.0 fusion.45
  458.2 5.8 %cholesky.81 = f32[64,64]{1,0:T(8,128)S(1)} custom-call(f32[64,64]{1,0:T(8,128)S(1)} %fusion.51), custom_call_target="Cholesky" | custom-call | tf_op jit(solution)/shard_map/jit(cholesky)/cholesky | solution.py:11
  464.1 0.6 compare_reduce_fusion
  464.7 0.7 fusion.43
  465.4 4.9 %custom-call.17 = f32[1,64,64]{1,2,0:T(8,128)S(1)} custom-call(f32[1,64,64]{2,1,0:T(8,128)S(1)} %fusion.43), custom_call_target="InvertDiagBlocksLowerTriangular" | custom-call | tf_op jit(solution)/shard_map/triangular_solve/custom-call.2 | solution.py:13
  470.3 0.2 fusion.47
  471.0 0.2 fusion.81
  471.2 0.4 convolution_bitcast_fusion
  471.7 0.7 fusion.103
  (82 shorter events, 5.6 us)
Async XLA Ops:
  7.2 93.9 %copy-start = (f32[2,4,128,128]{3,2,1,0:T(8,128)S(1)}, f32[2,4,128,128]{3,2,1,0:T(8,128)}, u32[]{:S(2)}) copy-start(f32[2,4,128,128]{3,2,1,0:T(8,128)} %param.19) | copy-start | bytes 1572868
  7.2 108.4 %reduce-scatter.3.cloned.1.call-start = ((), (), s32[]{:S(2)}) async-start(), calls=%async_computation.4 | async-start | bytes 4325376 | tf_op jit(solution)/shard_map/reduce_scatter | solution.py:85
  9.0 0.6 copy-start.9
  22.8 0.9 copy-start.3
  26.2 64.7 %all-to-all-start = ((f32[32,4,64,128]{3,2,1,0:T(8,128)}), f32[32,4,64,128]{3,2,1,0:T(8,128)}, u32[]{:S(2)}, u32[]{:S(2)}) async-start(f32[32,4,64,128]{3,2,1,0:T(8,128)} %stack.14), calls=%async_computation | async-start | bytes 8388608 | tf_op jit(solution)/shard_map/all_to_all | solution.py:35
  35.9 59.0 %copy-start.1 = (f32[4,11,128,128]{3,2,1,0:T(8,128)S(1)}, f32[4,11,128,128]{3,2,1,0:T(8,128)}, u32[]{:S(2)}) copy-start(f32[4,11,128,128]{3,2,1,0:T(8,128)} %param.18) | copy-start | bytes 8650756
  94.9 4.9 %copy-start.6 = (f32[4,128,128]{2,1,0:T(8,128)S(1)}, f32[4,128,128]{2,1,0:T(8,128)}, u32[]{:S(2)}) copy-start(f32[4,128,128]{2,1,0:T(8,128)} %param.17) | copy-start | bytes 786436
  94.9 6.2 %copy-start.5 = (f32[8,64,128]{2,1,0:T(8,128)S(1)}, f32[8,64,128]{2,1,0:T(8,128)}, u32[]{:S(2)}) copy-start(f32[8,64,128]{2,1,0:T(8,128)} %all_gather.6) | copy-start | bytes 786436
  119.1 7.6 %copy-start.10 = (s32[4,11]{1,0:T(4,128)S(1)}, s32[4,11]{1,0:T(4,128)}, u32[]{:S(2)}) copy-start(s32[4,11]{1,0:T(4,128)} %copy-done.9) | copy-start | bytes 532
  119.1 58.2 %all-to-all-start.1 = ((f32[32,4,64,128]{3,2,1,0:T(8,128)}), f32[32,4,64,128]{3,2,1,0:T(8,128)}, u32[]{:S(2)}, u32[]{:S(2)}) async-start(f32[32,4,64,128]{3,2,1,0:T(8,128)} %stack.15), calls=%async_computation.2 | async-start | bytes 8388608 | tf_op jit(solution)/shard_map/all_to_all | solution.py:35
  126.6 150.8 %reduce-scatter.5.cloned.1.call-start = ((), (), s32[]{:S(2)}) async-start(), calls=%async_computation.5 | async-start | bytes 4325376 | tf_op jit(solution)/shard_map/reduce_scatter | solution.py:89
  181.3 4.9 %copy-start.7 = (f32[4,128,128]{2,1,0:T(8,128)S(1)}, f32[4,128,128]{2,1,0:T(8,128)}, u32[]{:S(2)}) copy-start(f32[4,128,128]{2,1,0:T(8,128)} %param.17) | copy-start | bytes 786436
  181.3 5.6 %copy-start.4 = (f32[8,64,128]{2,1,0:T(8,128)S(1)}, f32[8,64,128]{2,1,0:T(8,128)}, u32[]{:S(2)}) copy-start(f32[8,64,128]{2,1,0:T(8,128)} %all_gather.7) | copy-start | bytes 786436
  181.3 6.2 %copy-start.2 = (f32[4,11,128,64]{2,3,1,0:T(8,128)S(1)}, f32[4,11,128,64]{2,3,1,0:T(8,128)}, u32[]{:S(2)}) copy-start(f32[4,11,128,64]{2,3,1,0:T(8,128)} %fusion.2) | copy-start | bytes 4325380
  197.1 228.7 %all-reduce.2.cloned.1.call-start = ((), (), s32[]{:S(2)}) async-start(), calls=%async_computation.6 | async-start | bytes 262144 | tf_op jit(solution)/shard_map/psum | solution.py:94
  278.6 192.6 %copy-start.8 = (f32[4,64,128]{2,1,0:T(8,128)S(1)}, f32[4,64,128]{2,1,0:T(8,128)}, u32[]{:S(2)}) copy-start(f32[4,64,128]{2,1,0:T(8,128)} %reduce-scatter.5.cloned.1.call-done) | copy-start | bytes 393220
Sparse Core Ops, SparseCore 0:
  23.0 92.6 reduce-scatter.2
  197.2 80.1 reduce-scatter.4
  282.7 143.0 all-reduce.1
